TPU v7x, 32 devices: a whole 2x2x4 slice. The times are simulated.
32 devices in a mesh: groups: 2 (over x), tokens: 16 (over z, y, core).
Axes of the slice: x: 2, y: 2, z: 4, core: 2. Of those that a mesh axis runs over, the one named last changes fastest.
Arguments:
- update_keys: bfloat16 [16384, 2048], P(('groups', 'tokens')), parts along dimension 0, may hold values from -6 to 6
- update_values: bfloat16 [16384, 2048], P(('groups', 'tokens')), parts along dimension 0, may hold values from -6 to 6
- update_rates: float32 [16384, 4], P(('groups', 'tokens')), parts along dimension 0, may hold values from 0.05 to 1
- update_mask: int32 [16384], P(('groups', 'tokens')), parts along dimension 0, may hold values 0 or 1
- fast_weights: bfloat16 [4, 3, 512, 512], replicated, may hold values from -0.25 to 0.25
- step_sizes: float32 [4], replicated, may hold values from 0.02 to 0.08
- target_queries: bfloat16 [4096, 2048], P(('groups', 'tokens')), parts along dimension 0, may hold values from -8 to 8
- target_keys: bfloat16 [4096, 2048], P(('groups', 'tokens')), parts along dimension 0, may hold values from -8 to 8
- target_values: bfloat16 [4096, 2048], P(('groups', 'tokens')), parts along dimension 0, may hold values from -6 to 6
- target_views: int32 [4096], P(('groups', 'tokens')), parts along dimension 0, may hold values from 0 to 15, as said below
Outputs:
- mixed: bfloat16 [4096, 2048], P(('groups', 'tokens')), parts along dimension 0
There are 2 independent parts, one for each index of `groups`. A program takes and returns all parts, laid end to end along the dimension named above; an argument that names none is the same for every part. Nothing has to cross between parts.
Inputs may be any that keep to these rules, and one draw needn't show every extreme that they name: `target_views`: every view id names exactly 128 rows. Owner o holds view o; of the 128 rows of one device, either none or exactly 16 belong to the view of one owner.
All inputs are finite; a program needn't handle non-finite values. No bound on the sum of `update_mask` on one device may be relied on, other than what follows from the above.
Results may differ from a plain program's by a relative error of at most 0.0083.
Values may be sent and summed in bfloat16 or wider, within the bound.
A program may use at most 128 MiB of HBM per device.

v0:
```python
import jax
import jax.numpy as jnp
from jax import lax
from jax.sharding import PartitionSpec as P

VIEW_ROWS = 128
VIEWS_DEV = 1


epsilon = 1e-05


def swish_parts(pre_gate):
    sigma = jax.nn.sigmoid(pre_gate)
    return (pre_gate * sigma, sigma * (1.0 + pre_gate * (1.0 - sigma)))


def row_normalize(matrix):
    return matrix * lax.rsqrt(jnp.mean(matrix * matrix, axis=-1, keepdims=True) + epsilon)


def local_gradient(update_keys, update_values, update_rates, update_mask, fast_weights):
    row_count = update_keys.shape[0]
    head_count = fast_weights.shape[0]
    head_width = fast_weights.shape[2]
    key_rows = update_keys.reshape(row_count, head_count, head_width)
    rate_rows = update_mask.astype(jnp.float32)[:, None] * update_rates
    value_rows = update_values.reshape(row_count, head_count, head_width).astype(jnp.float32)
    target_grad = (-rate_rows[:, :, None] * value_rows).astype(jnp.bfloat16)
    pre_gate = jnp.einsum(
        "rhi,hij->rhj", key_rows, fast_weights[:, 0], preferred_element_type=jnp.float32
    )
    pre_up = jnp.einsum(
        "rhi,hij->rhj", key_rows, fast_weights[:, 1], preferred_element_type=jnp.float32
    )
    activated, slope = swish_parts(pre_gate)
    hidden = (activated * pre_up).astype(jnp.bfloat16)
    back = jnp.einsum(
        "rho,hjo->rhj", target_grad, fast_weights[:, 2], preferred_element_type=jnp.float32
    )
    grad_gate = (back * pre_up * slope).astype(jnp.bfloat16)
    grad_up = (back * activated).astype(jnp.bfloat16)
    gate_term = jnp.einsum("rhi,rhj->hij", key_rows, grad_gate, preferred_element_type=jnp.float32)
    up_term = jnp.einsum("rhi,rhj->hij", key_rows, grad_up, preferred_element_type=jnp.float32)
    down_term = jnp.einsum("rhj,rho->hjo", hidden, target_grad, preferred_element_type=jnp.float32)
    return jnp.stack([gate_term, up_term, down_term], axis=1)


def update_weights(update_keys, update_values, update_rates, update_mask, fast_weights, step_sizes):
    grad_local = local_gradient(update_keys, update_values, update_rates, update_mask, fast_weights)
    head_count = fast_weights.shape[0]
    head_width = fast_weights.shape[2]
    flat_rows = 3 * head_count * head_width
    grad_share = lax.psum_scatter(
        grad_local.reshape(flat_rows, head_width), "tokens", scatter_dimension=0, tiled=True
    )
    share_rows = grad_share.shape[0]
    first_row = lax.axis_index("tokens") * share_rows
    own_rows = lax.dynamic_slice_in_dim(
        fast_weights.reshape(flat_rows, head_width), first_row, share_rows, 0
    )
    head_of_row = (first_row + jnp.arange(share_rows, dtype=jnp.int32)) // (3 * head_width)
    head_match = head_of_row[:, None] == jnp.arange(head_count, dtype=jnp.int32)[None, :]
    step_rows = jnp.sum(jnp.where(head_match, step_sizes[None, :], 0.0), axis=1)
    fresh_share = (
        own_rows.astype(jnp.float32) - step_rows[:, None] * row_normalize(grad_share)
    ).astype(jnp.bfloat16)
    fresh = lax.all_gather(fresh_share, "tokens", axis=0, tiled=True).reshape(
        head_count, 3, head_width, head_width
    )
    return fresh


def regroup_rows(target_queries, target_keys, target_values, target_views):
    row_count = target_views.shape[0]
    dev_count = lax.axis_size("tokens")
    capacity = 2 * row_count // dev_count
    owner_dev = target_views // VIEWS_DEV
    hit_int = (owner_dev[:, None] == jnp.arange(dev_count, dtype=jnp.int32)[None, :]).astype(
        jnp.int32
    )
    dev_rank = jnp.sum(hit_int * (jnp.cumsum(hit_int, axis=0) - 1), axis=1)
    slot_index = owner_dev * capacity + dev_rank
    pick_hit = jnp.arange(dev_count * capacity, dtype=jnp.int32)[:, None] == slot_index[None, :]
    pick_table = pick_hit.astype(jnp.bfloat16)
    sent_queries = jnp.dot(pick_table, target_queries, preferred_element_type=jnp.float32).astype(
        jnp.bfloat16
    )
    sent_keys = jnp.dot(pick_table, target_keys, preferred_element_type=jnp.float32).astype(
        jnp.bfloat16
    )
    sent_values = jnp.dot(pick_table, target_values, preferred_element_type=jnp.float32).astype(
        jnp.bfloat16
    )
    sent_views = jnp.sum(jnp.where(pick_hit, target_views[None, :] + 1, 0), axis=1) - 1
    got_queries, got_keys, got_values, got_views = (
        lax.all_to_all(sent_queries, "tokens", split_axis=0, concat_axis=0, tiled=True),
        lax.all_to_all(sent_keys, "tokens", split_axis=0, concat_axis=0, tiled=True),
        lax.all_to_all(sent_values, "tokens", split_axis=0, concat_axis=0, tiled=True),
        lax.all_to_all(sent_views, "tokens", split_axis=0, concat_axis=0, tiled=True),
    )
    is_valid = got_views >= 0
    local_view = jnp.where(is_valid, got_views % VIEWS_DEV, 0)
    view_match = is_valid[:, None] & (
        local_view[:, None] == jnp.arange(VIEWS_DEV, dtype=jnp.int32)[None, :]
    )
    view_hit = view_match.astype(jnp.int32)
    view_rank = jnp.sum(view_hit * (jnp.cumsum(view_hit, axis=0) - 1), axis=1)
    placed_at = jnp.where(is_valid, local_view * VIEW_ROWS + view_rank, -1)
    place_table = (jnp.arange(row_count, dtype=jnp.int32)[:, None] == placed_at[None, :]).astype(
        jnp.bfloat16
    )
    return tuple(
        (
            jnp.dot(place_table, got_rows, preferred_element_type=jnp.float32).astype(jnp.bfloat16)
            for got_rows in (got_queries, got_keys, got_values)
        )
    )


def attend_views(arranged, head_count, head_width):
    row_count = arranged[0].shape[0]
    view_shape = (row_count // VIEW_ROWS, VIEW_ROWS, head_count, head_width)
    scores = jnp.einsum(
        "vqhd,vkhd->vhqk",
        arranged[0].reshape(view_shape),
        arranged[1].reshape(view_shape),
        preferred_element_type=jnp.float32,
    ) * head_width ** (-0.5)
    probs = jax.nn.softmax(scores, axis=-1).astype(jnp.bfloat16)
    attended = jnp.einsum(
        "vhqk,vkhd->vqhd",
        probs,
        arranged[2].reshape(view_shape),
        preferred_element_type=jnp.float32,
    )
    return attended.reshape(row_count, head_count, head_width)


def finish_rows(fresh, arranged_queries, attended):
    row_count = arranged_queries.shape[0]
    head_count = fresh.shape[0]
    head_width = fresh.shape[2]
    query_rows = arranged_queries.reshape(row_count, head_count, head_width)
    pre_gate = jnp.einsum(
        "rhi,hij->rhj", query_rows, fresh[:, 0], preferred_element_type=jnp.float32
    )
    pre_up = jnp.einsum("rhi,hij->rhj", query_rows, fresh[:, 1], preferred_element_type=jnp.float32)
    activated, slope = swish_parts(pre_gate)
    target_hidden = (activated * pre_up).astype(jnp.bfloat16)
    fast_out = jnp.einsum(
        "rhj,hjo->rho", target_hidden, fresh[:, 2], preferred_element_type=jnp.float32
    )
    mixed = row_normalize(fast_out) + attended
    return mixed.reshape(row_count, head_count * head_width).astype(jnp.bfloat16)


def on_device(
    update_keys,
    update_values,
    update_rates,
    update_mask,
    fast_weights,
    step_sizes,
    target_queries,
    target_keys,
    target_values,
    target_views,
):
    head_count = fast_weights.shape[0]
    head_width = fast_weights.shape[2]
    fresh = update_weights(
        update_keys, update_values, update_rates, update_mask, fast_weights, step_sizes
    )
    arranged = regroup_rows(target_queries, target_keys, target_values, target_views)
    attended = attend_views(arranged, head_count, head_width)
    return finish_rows(fresh, arranged[0], attended)


def solution(mesh):
    return jax.shard_map(
        on_device,
        mesh=mesh,
        in_specs=(
            P(("groups", "tokens"), None),
            P(("groups", "tokens"), None),
            P(("groups", "tokens"), None),
            P(("groups", "tokens")),
            P(),
            P(),
            P(("groups", "tokens"), None),
            P(("groups", "tokens"), None),
            P(("groups", "tokens"), None),
            P(("groups", "tokens")),
        ),
        out_specs=P(("groups", "tokens"), None),
        check_vma=False,
    )
```

profile of v0, /device:TPU:0, one launch (start us, length us, event | category | flops | bytes accessed | tf_op | source)
XLA Modules:
  0.0 328.3 jit_solution(13886927430357881111)
XLA Ops:
  6.5 2.9 copy.131
  9.5 3.0 fusion.16
  12.5 0.4 copy-done.1
  12.9 1.3 fusion.18
  14.5 0.5 convert_element_type.100
  15.1 1.6 fusion.20
  16.6 3.5 %convolution_bitcast_fusion.2 = f32[4,1,512,512]{3,2,0,1:T(8,128)} fusion(f32[4,512,512]{1,2,0:T(8,128)S(1)} %fusion.18, f32[4,512,512]{1,2,0:T(8,128)S(1)} %fusion.16, f32[64,4,8,512]{3,2,1,0:T(8,128)S(1)} %bitcast.183, f32[512,4]{0,1:T(4,128)S(1)} %multiply_negate_fusion), kind=kOutput, calls=%fused_computation.27 | convolution fusion | flops 1082130432 | bytes 16785408 | tf_op jit(solution)/shard_map/rhj,rho->hjo/dot_general | solution.py:45
  20.1 4.0 %convolution_bitcast_fusion.1 = f32[4,1,512,512]{3,2,0,1:T(8,128)} fusion(bf16[512,4,512]{0,2,1:T(8,128)(2,1)S(1)} %bitcast.180, f32[4,512,512]{1,2,0:T(8,128)S(1)} %fusion.16, f32[4,512,512]{1,2,0:T(8,128)S(1)} %fusion.18, f32[4,512,512]{2,1,0:T(8,128)S(1)} %fusion.20), kind=kOutput, calls=%fused_computation.26 | convolution fusion | flops 1084227584 | bytes 18874368 | tf_op jit(solution)/shard_map/rhi,rhj->hij/dot_general | solution.py:43
  24.1 3.4 %convolution_bitcast_fusion = f32[4,1,512,512]{3,2,0,1:T(8,128)} fusion(bf16[512,4,512]{0,2,1:T(8,128)(2,1)S(1)} %bitcast.181, f32[4,512,512]{2,1,0:T(8,128)S(1)} %fusion.20, f32[4,512,512]{1,2,0:T(8,128)S(1)} %fusion.16), kind=kOutput, calls=%fused_computation.25 | convolution fusion | flops 1080033280 | bytes 14680064 | tf_op jit(solution)/shard_map/rhi,rhj->hij/dot_general | solution.py:44
  27.5 10.7 %pad_maximum_fusion = f32[4,3,512,512]{3,2,0,1:T(8,128)} fusion(f32[4,1,512,512]{3,2,0,1:T(8,128)} %convolution_bitcast_fusion.2, f32[4,1,512,512]{3,2,0,1:T(8,128)} %convolution_bitcast_fusion, f32[4,1,512,512]{3,2,0,1:T(8,128)} %convolution_bitcast_fusion.1), kind=kLoop, calls=%fused_computation.1 | loop fusion | flops 6291456 | bytes 25165824 | tf_op jit(solution)/shard_map/stack | solution.py:46
  38.2 10.6 %copy.107 = f32[4,3,512,512]{3,2,1,0:T(8,128)} copy(f32[4,3,512,512]{3,2,0,1:T(8,128)} %pad_maximum_fusion) | data formatting | bytes 25165824 | tf_op jit(solution)/shard_map/stack | solution.py:46
  48.9 0.5 copy-done.8
  49.6 137.0 %reduce-scatter.2.cloned.1.call-done = f32[384,512]{1,0:T(8,128)} async-done(((f32[6144,512]{1,0:T(8,128)}), f32[384,512]{1,0:T(8,128)}) %reduce-scatter.2.cloned.1.call-update) | async-done | bytes 786448 | tf_op jit(solution)/shard_map/reduce_scatter | solution.py:54
  186.6 1.3 multiply_reduce_fusion.1
  187.9 2.2 subtract_convert_fusion
  190.7 0.7 sub.44
  191.4 4.2 %all-to-all-start = ((s32[16,16,1]{1,2,0:T(1,128)}), s32[16,16,1]{1,2,0:T(1,128)S(1)}, u32[]{:S(2)}, u32[]{:S(2)}) async-start(s32[16,16,1]{1,2,0:T(1,128)} %sub.44), calls=%async_computation.1 | async-start | bytes 16384 | tf_op jit(solution)/shard_map/all_to_all | solution.py:100
  195.6 1.4 convolution_convert_fusion
  197.0 5.0 %all-to-all-done = s32[16,16,1]{1,2,0:T(1,128)S(1)} async-done(((s32[16,16,1]{1,2,0:T(1,128)}), s32[16,16,1]{1,2,0:T(1,128)S(1)}, u32[]{:S(2)}, u32[]{:S(2)}) %all-to-all-start) | async-done | bytes 1056 | tf_op jit(solution)/shard_map/all_to_all | solution.py:100
  202.0 3.7 %all-to-all-start.3 = ((bf16[16,16,2048]{2,1,0:T(8,128)(2,1)}), bf16[16,16,2048]{2,1,0:T(8,128)(2,1)S(1)}, u32[]{:S(2)}, u32[]{:S(2)}) async-start(bf16[16,16,2048]{2,1,0:T(8,128)(2,1)} %bitcast.28), calls=%async_computation.4 | async-start | bytes 2097152 | tf_op jit(solution)/shard_map/all_to_all | solution.py:98
  205.7 1.4 convolution_convert_fusion.1
  207.1 31.1 %all-to-all-done.3 = bf16[16,16,2048]{2,1,0:T(8,128)(2,1)S(1)} async-done(((bf16[16,16,2048]{2,1,0:T(8,128)(2,1)}), bf16[16,16,2048]{2,1,0:T(8,128)(2,1)S(1)}, u32[]{:S(2)}, u32[]{:S(2)}) %all-to-all-start.3) | async-done | bytes 1048608 | tf_op jit(solution)/shard_map/all_to_all | solution.py:98
  238.2 17.5 %all-to-all-start.2 = ((bf16[16,16,2048]{2,1,0:T(8,128)(2,1)}), bf16[16,16,2048]{2,1,0:T(8,128)(2,1)S(1)}, u32[]{:S(2)}, u32[]{:S(2)}) async-start(bf16[16,16,2048]{2,1,0:T(8,128)(2,1)} %bitcast.188), calls=%async_computation.3 | async-start | bytes 2097152 | tf_op jit(solution)/shard_map/all_to_all | solution.py:99
  255.7 1.4 convolution_convert_fusion.2
  257.1 24.0 %all-to-all-done.2 = bf16[16,16,2048]{2,1,0:T(8,128)(2,1)S(1)} async-done(((bf16[16,16,2048]{2,1,0:T(8,128)(2,1)}), bf16[16,16,2048]{2,1,0:T(8,128)(2,1)S(1)}, u32[]{:S(2)}, u32[]{:S(2)}) %all-to-all-start.2) | async-done | bytes 1048608 | tf_op jit(solution)/shard_map/all_to_all | solution.py:99
  281.1 6.5 %all-to-all-start.1 = ((bf16[16,16,2048]{2,1,0:T(8,128)(2,1)}), bf16[16,16,2048]{2,1,0:T(8,128)(2,1)}, u32[]{:S(2)}, u32[]{:S(2)}) async-start(bf16[16,16,2048]{2,1,0:T(8,128)(2,1)} %bitcast.187), calls=%async_computation.2 | async-start | bytes 2097152 | tf_op jit(solution)/shard_map/all_to_all | solution.py:97
  289.6 21.0 %all-to-all-done.1 = bf16[16,16,2048]{2,1,0:T(8,128)(2,1)} async-done(((bf16[16,16,2048]{2,1,0:T(8,128)(2,1)}), bf16[16,16,2048]{2,1,0:T(8,128)(2,1)}, u32[]{:S(2)}, u32[]{:S(2)}) %all-to-all-start.1) | async-done | bytes 1048608 | tf_op jit(solution)/shard_map/all_to_all | solution.py:97
  310.6 1.5 convolution_convert_fusion.5
  312.6 3.5 %fusion.27 = f32[128,4,512]{0,2,1:T(8,128)} fusion(bf16[4,3,512,512]{3,2,1,0:T(8,128)(2,1)} %bitcast.196, bf16[16,4,8,512]{3,2,1,0:T(8,128)(2,1)S(1)} %bitcast.192), kind=kOutput, calls=%fused_computation.44 | convolution fusion | flops 268435456 | bytes 3670016 | tf_op jit(solution)/shard_map/rhi,hij->rhj/dot_general | solution.py:145
  316.1 4.1 %multiply_reduce_fusion = (f32[128,4]{0,1:T(4,128)S(1)}, f32[128,4,512]{0,2,1:T(8,128)S(1)}) fusion(bf16[4,3,512,512]{3,2,1,0:T(8,128)(2,1)} %bitcast.197, f32[128,4,512]{0,2,1:T(8,128)} %fusion.27, bf16[16,4,8,512]{3,2,1,0:T(8,128)(2,1)S(1)} %bitcast.193), kind=kOutput, calls=%fused_computation.54 | convolution fusion | flops 538967552 | bytes 6817792 | tf_op jit(solution)/shard_map/rhj,hjo->rho/dot_general | solution.py:151
  320.1 0.3 fusion.32
  320.5 1.0 copy.118
  (48 shorter events, 3.3 us)
Async XLA Ops:
  6.5 189.0 %copy-start = (bf16[128,2048]{1,0:T(8,128)(2,1)S(1)}, bf16[128,2048]{1,0:T(8,128)(2,1)}, u32[]{:S(2)}) copy-start(bf16[128,2048]{1,0:T(8,128)(2,1)} %param.17) | copy-start | bytes 1572868
  6.5 180.1 %reduce-scatter.2.cloned.1.call-start = ((), (), s32[]{:S(2)}) async-start(), calls=%async_computation.5 | async-start | bytes 13369344 | tf_op jit(solution)/shard_map/reduce_scatter | solution.py:54
  9.5 3.4 %copy-start.1 = (bf16[4,3,512,512]{3,2,1,0:T(8,128)(2,1)S(1)}, bf16[4,3,512,512]{3,2,1,0:T(8,128)(2,1)}, u32[]{:S(2)}) copy-start(bf16[4,3,512,512]{3,2,1,0:T(8,128)(2,1)} %param.14) | copy-start | bytes 18874372
  12.9 1.3 copy-start.7
  12.9 1.6 copy-start.2
  14.2 0.8 copy-start.5
  48.8 0.7 copy-start.8
  48.8 141.3 %copy-start.6 = (s32[128]{0:T(128)S(1)}, s32[128]{0:T(128)}, u32[]{:S(2)}) copy-start(s32[128]{0:T(128)} %param.19) | copy-start | bytes 1540
  48.8 156.8 %copy-start.3 = (bf16[128,2048]{1,0:T(8,128)(2,1)S(1)}, bf16[128,2048]{1,0:T(8,128)(2,1)}, u32[]{:S(2)}) copy-start(bf16[128,2048]{1,0:T(8,128)(2,1)} %param.18) | copy-start | bytes 1572868
  48.9 263.7 %all-gather.2.cloned.1.call-start = ((), (), s32[]{:S(2)}) async-start(), calls=%async_computation.6 | async-start | bytes 6684672 | tf_op jit(solution)/shard_map/all_gather | solution.py:68
  190.1 65.6 %copy-start.4 = (bf16[128,2048]{1,0:T(8,128)(2,1)S(1)}, bf16[128,2048]{1,0:T(8,128)(2,1)}, u32[]{:S(2)}) copy-start(bf16[128,2048]{1,0:T(8,128)(2,1)} %param.16) | copy-start | bytes 1572868
  191.4 10.6 %all-to-all-start = ((s32[16,16,1]{1,2,0:T(1,128)}), s32[16,16,1]{1,2,0:T(1,128)S(1)}, u32[]{:S(2)}, u32[]{:S(2)}) async-start(s32[16,16,1]{1,2,0:T(1,128)} %sub.44), calls=%async_computation.1 | async-start | bytes 16384 | tf_op jit(solution)/shard_map/all_to_all | solution.py:100
  202.0 36.2 %all-to-all-start.3 = ((bf16[16,16,2048]{2,1,0:T(8,128)(2,1)}), bf16[16,16,2048]{2,1,0:T(8,128)(2,1)S(1)}, u32[]{:S(2)}, u32[]{:S(2)}) async-start(bf16[16,16,2048]{2,1,0:T(8,128)(2,1)} %bitcast.28), calls=%async_computation.4 | async-start | bytes 2097152 | tf_op jit(solution)/shard_map/all_to_all | solution.py:98
  238.2 42.9 %all-to-all-start.2 = ((bf16[16,16,2048]{2,1,0:T(8,128)(2,1)}), bf16[16,16,2048]{2,1,0:T(8,128)(2,1)S(1)}, u32[]{:S(2)}, u32[]{:S(2)}) async-start(bf16[16,16,2048]{2,1,0:T(8,128)(2,1)} %bitcast.188), calls=%async_computation.3 | async-start | bytes 2097152 | tf_op jit(solution)/shard_map/all_to_all | solution.py:99
  281.1 29.5 %all-to-all-start.1 = ((bf16[16,16,2048]{2,1,0:T(8,128)(2,1)}), bf16[16,16,2048]{2,1,0:T(8,128)(2,1)}, u32[]{:S(2)}, u32[]{:S(2)}) async-start(bf16[16,16,2048]{2,1,0:T(8,128)(2,1)} %bitcast.187), calls=%async_computation.2 | async-start | bytes 2097152 | tf_op jit(solution)/shard_map/all_to_all | solution.py:97
Sparse Core Ops, SparseCore 0:
  49.0 137.5 reduce-scatter.1
  190.2 87.0 all-gather.1
where the time goes:
time: 330 us; the launch traced here: 328 us
  waiting for transfers between devices  218 us (66%)
  starting transfers between devices  31.9 us (10%)
  matrix products  31.3 us (9%)
  local copies, waits for them, and re-layouts  17.1 us (5%)
  other arithmetic  16.1 us (5%)
  between operations  13.7 us (4%)
    reduce_scatter x1, waiting for transfers between devices, update_weights(): lax.psum_scatter(grad_local.reshape(flat_rows, head_width), 'tokens', sca...  137 us
    all_to_all x1, waiting for transfers between devices, regroup_rows(): lax.all_to_all(sent_keys, 'tokens', split_axis=0, concat_axis=0, tiled=True)  31.1 us
    all_to_all x1, waiting for transfers between devices, regroup_rows(): lax.all_to_all(sent_values, 'tokens', split_axis=0, concat_axis=0, tiled=...  24 us
    all_to_all x1, waiting for transfers between devices, regroup_rows(): lax.all_to_all(sent_queries, 'tokens', split_axis=0, concat_axis=0, tiled...  21 us
    all_to_all x1, starting transfers between devices, regroup_rows(): lax.all_to_all(sent_values, 'tokens', split_axis=0, concat_axis=0, tiled=...  17.5 us
    another operation x1, other arithmetic, local_gradient(): return jnp.stack([gate_term, up_term, down_term], axis=1)  10.7 us
    another operation x1, local copies, waits for them, and re-layouts, local_gradient(): return jnp.stack([gate_term, up_term, down_term], axis=1)  10.6 us
  transfers between devices with their start and end apart: 6, of which 5 were waited for; matrix products, arithmetic and copies ran while one was open for 3% of the time, Pallas kernels for 0%

commit v1 on v0

v1 whole, which is shorter than its diff:
```python
import functools
import math

import jax
import jax.numpy as jnp
from jax import lax
from jax.experimental import pallas as pl
from jax.experimental.pallas import tpu as pltpu
from jax.sharding import PartitionSpec as P

EPS = 1e-05
VIEW_ROWS = 128
MESH = pl.DeviceIdType.MESH
F32 = jnp.float32
BF16 = jnp.bfloat16


def remote(src, dst, send_sem, recv_sem, peer):
    return pltpu.make_async_remote_copy(
        src_ref=src,
        dst_ref=dst,
        send_sem=send_sem,
        recv_sem=recv_sem,
        device_id={"tokens": peer},
        device_id_type=MESH,
    )


def exchange_kernel(
    n,
    heads,
    keys_ref,
    values_ref,
    rates_ref,
    weights_ref,
    steps_ref,
    packed_ref,
    meta_ref,
    fresh_ref,
    got_ref,
    got_meta_ref,
    grad,
    core_out,
    core_in,
    side_out,
    side_in,
    up_out,
    up_in,
    down_out,
    down_in,
    a2a_send,
    a2a_recv,
    meta_send,
    meta_recv,
    pair_send,
    pair_recv,
    chain_send,
    chain_recv,
    spread_send,
    spread_recv,
):
    width = weights_ref.shape[-1]
    quads = n // heads
    piece = 3 * width // quads
    slots = packed_ref.shape[1] // quads
    me = lax.axis_index("tokens")
    quad = me // heads
    head = me % heads
    core = head % 2
    side = head // 2
    core_peer = me + 1 - 2 * core
    side_peer = me + 2 - 4 * side

    barrier = pltpu.get_barrier_semaphore()
    for step in range(1, n):
        pl.semaphore_signal(
            barrier, inc=1, device_id={"tokens": (me + step) % n}, device_id_type=MESH
        )
    pl.semaphore_wait(barrier, n - 1)

    def block_copy(step):
        peer = (me + step) % n
        rows = pl.ds(pl.multiple_of((peer // heads) * slots, slots), slots)
        columns = pl.ds(pl.multiple_of((peer % heads) * width, width), width)
        return remote(
            packed_ref.at[:, rows, columns],
            got_ref.at[me],
            a2a_send.at[step],
            a2a_recv.at[step],
            peer,
        )

    def meta_copy(step):
        peer = (me + step) % n
        return remote(
            meta_ref, got_meta_ref.at[me], meta_send.at[step], meta_recv.at[step], peer
        )

    for step in range(1, n):
        meta_copy(step).start()
    for step in range(1, n):
        block_copy(step).start()
    got_meta_ref[me] = meta_ref[...]
    got_ref[me] = packed_ref[
        :,
        pl.ds(pl.multiple_of(quad * slots, slots), slots),
        pl.ds(pl.multiple_of(head * width, width), width),
    ]

    def core_copy(slot):
        return remote(
            core_out.at[slot], core_in.at[slot], pair_send.at[slot], pair_recv.at[slot], core_peer
        )

    side_copy = remote(side_out, side_in, pair_send.at[2], pair_recv.at[2], side_peer)

    def one_head(turn, carry):
        on_side = jnp.where(turn < 2, 1 - side, side)
        on_core = jnp.where(turn % 2 == 0, 1 - core, core)
        now = on_side * 2 + on_core
        columns = pl.ds(pl.multiple_of(now * width, width), width)
        key_rows = keys_ref[:, columns]
        rates = rates_ref[...]
        lanes = lax.broadcasted_iota(jnp.int32, rates.shape, 1)
        rate = jnp.sum(jnp.where(lanes == now, rates, 0.0), axis=1, keepdims=True)
        target_grad = (-rate * values_ref[:, columns].astype(F32)).astype(BF16)
        pre_gate = jnp.dot(key_rows, weights_ref[now, 0], preferred_element_type=F32)
        pre_up = jnp.dot(key_rows, weights_ref[now, 1], preferred_element_type=F32)
        back = lax.dot_general(
            target_grad,
            weights_ref[now, 2],
            (((1,), (1,)), ((), ())),
            preferred_element_type=F32,
        )
        sigma = jax.nn.sigmoid(pre_gate)
        activated = pre_gate * sigma
        hidden = (activated * pre_up).astype(BF16)
        grad_gate = (back * pre_up * sigma * (1.0 + pre_gate * (1.0 - sigma))).astype(BF16)
        grad_up = (back * activated).astype(BF16)
        over_rows = (((0,), (0,)), ((), ()))
        grad[0:width] = lax.dot_general(
            key_rows, grad_gate, over_rows, preferred_element_type=F32
        )
        grad[width : 2 * width] = lax.dot_general(
            key_rows, grad_up, over_rows, preferred_element_type=F32
        )
        grad[2 * width : 3 * width] = lax.dot_general(
            hidden, target_grad, over_rows, preferred_element_type=F32
        )

        @pl.when(turn == 0)
        def _():
            core_out[0] = grad[...].astype(BF16)
            core_copy(0).start()

        @pl.when(turn == 1)
        def _():
            core_copy(0).wait_recv()
            side_out[...] = (grad[...] + core_in[0].astype(F32)).astype(BF16)
            side_copy.start()

        @pl.when(turn == 2)
        def _():
            core_out[1] = grad[...].astype(BF16)
            core_copy(1).start()

        return carry

    lax.fori_loop(0, 4, one_head, 0)
    core_copy(1).wait_recv()
    side_copy.wait_recv()

    def rows_of(index):
        return pl.ds(index * piece, piece)

    def own_part(rows):
        return grad[rows, :] + core_in[1, rows, :].astype(F32) + side_in[rows, :].astype(F32)

    def up_copy(index):
        return remote(
            up_out.at[index],
            up_in.at[index],
            chain_send.at[0, index],
            chain_recv.at[0, index],
            me + heads,
        )

    def down_copy(index):
        return remote(
            down_out.at[index],
            down_in.at[index],
            chain_send.at[1, index],
            chain_recv.at[1, index],
            me - heads,
        )

    for turn in range(quads - 1):
        high = quads - 1 - turn
        low = turn

        @pl.when(quad == 0)
        def _():
            up_out[high] = own_part(rows_of(high)).astype(BF16)
            up_copy(high).start()

        @pl.when(quad == quads - 1)
        def _():
            down_out[low] = own_part(rows_of(low)).astype(BF16)
            down_copy(low).start()

        @pl.when((quad > 0) & (quad < high))
        def _():
            up_copy(high).wait_recv()
            up_out[high] = (own_part(rows_of(high)) + up_in[high].astype(F32)).astype(BF16)
            up_copy(high).start()

        @pl.when((quad < quads - 1) & (quad > low))
        def _():
            down_copy(low).wait_recv()
            down_out[low] = (own_part(rows_of(low)) + down_in[low].astype(F32)).astype(BF16)
            down_copy(low).start()

    mine = pl.ds(pl.multiple_of(quad * piece, piece), piece)
    grad[mine, :] = own_part(mine)

    @pl.when(quad > 0)
    def _():
        up_copy(quad).wait_recv()
        grad[mine, :] += up_in[quad].astype(F32)

    @pl.when(quad < quads - 1)
    def _():
        down_copy(quad).wait_recv()
        grad[mine, :] += down_in[quad].astype(F32)

    total = grad[mine, :]
    scaled = total * lax.rsqrt(jnp.mean(total * total, axis=-1, keepdims=True) + EPS)
    first = quad * piece
    block = math.gcd(piece, width)
    for part in range(piece // block):
        start = first + part * block
        old = weights_ref[
            head, start // width, pl.ds(pl.multiple_of(start % width, block), block), :
        ]
        fresh_ref[quad, part * block : (part + 1) * block, :] = (
            old.astype(F32) - steps_ref[head] * scaled[part * block : (part + 1) * block, :]
        ).astype(BF16)

    def spread_copy(way, index):
        return remote(
            fresh_ref.at[index],
            fresh_ref.at[index],
            spread_send.at[way, index],
            spread_recv.at[index],
            me + heads if way == 0 else me - heads,
        )

    @pl.when(quad < quads - 1)
    def _():
        spread_copy(0, quad).start()

    @pl.when(quad > 0)
    def _():
        spread_copy(1, quad).start()

    for hop in range(1, quads):

        @pl.when(quad - hop >= 0)
        def _():
            index = quad - hop
            spread_copy(0, index).wait_recv()

            @pl.when(quad < quads - 1)
            def _():
                spread_copy(0, index).start()

        @pl.when(quad + hop < quads)
        def _():
            index = quad + hop
            spread_copy(1, index).wait_recv()

            @pl.when(quad > 0)
            def _():
                spread_copy(1, index).start()

    core_copy(0).wait_send()
    core_copy(1).wait_send()
    side_copy.wait_send()
    for index in range(quads):

        @pl.when(quad < index)
        def _():
            up_copy(index).wait_send()

        @pl.when(quad > index)
        def _():
            down_copy(index).wait_send()

        @pl.when((index <= quad) & (quad < quads - 1))
        def _():
            spread_copy(0, index).wait_send()

        @pl.when((index >= quad) & (quad > 0))
        def _():
            spread_copy(1, index).wait_send()

    for step in range(1, n):
        meta_copy(step).wait()
        block_copy(step).wait()


def exchange(keys, values, rates, weights, steps, packed, meta):
    n = lax.axis_size("tokens")
    heads = weights.shape[0]
    width = weights.shape[-1]
    quads = n // heads
    piece = 3 * width // quads
    slots = packed.shape[1] // quads
    rows = keys.shape[0]
    vmem = pl.BlockSpec(memory_space=pltpu.VMEM)
    smem = pl.BlockSpec(memory_space=pltpu.SMEM)
    dma = pltpu.SemaphoreType.DMA
    whole = (3 * width, width)
    parts = (quads, piece, width)
    return pl.pallas_call(
        functools.partial(exchange_kernel, n, heads),
        out_shape=(
            jax.ShapeDtypeStruct(parts, BF16),
            jax.ShapeDtypeStruct((n, 3, slots, width), BF16),
            jax.ShapeDtypeStruct((n,) + meta.shape, jnp.int32),
        ),
        in_specs=[vmem, vmem, vmem, vmem, smem, vmem, vmem],
        out_specs=(vmem, vmem, vmem),
        scratch_shapes=[
            pltpu.VMEM(whole, F32),
            pltpu.VMEM((2,) + whole, BF16),
            pltpu.VMEM((2,) + whole, BF16),
            pltpu.VMEM(whole, BF16),
            pltpu.VMEM(whole, BF16),
            pltpu.VMEM(parts, BF16),
            pltpu.VMEM(parts, BF16),
            pltpu.VMEM(parts, BF16),
            pltpu.VMEM(parts, BF16),
            dma((n,)),
            dma((n,)),
            dma((n,)),
            dma((n,)),
            dma((3,)),
            dma((3,)),
            dma((2, quads)),
            dma((2, quads)),
            dma((2, quads)),
            dma((quads,)),
        ],
        compiler_params=pltpu.CompilerParams(
            collective_id=0, has_side_effects=True, vmem_limit_bytes=63 * 1024 * 1024
        ),
    )(keys, values, rates, weights, steps, packed, meta)


def pack_rows(queries, keys, values, views, n):
    rows = views.shape[0]
    capacity = 2 * rows // n
    hits = (views[:, None] // (rows // VIEW_ROWS) == jnp.arange(n, dtype=jnp.int32)[None, :]).astype(
        jnp.int32
    )
    before = jnp.tril(jnp.ones((rows, rows), BF16), -1)
    rank = jnp.sum(
        hits * jnp.dot(before, hits.astype(BF16), preferred_element_type=F32).astype(jnp.int32),
        axis=1,
    )
    slot = (views // (rows // VIEW_ROWS)) * capacity + rank
    pick = (jnp.arange(n * capacity, dtype=jnp.int32)[:, None] == slot[None, :]).astype(BF16)
    packed = jnp.stack(
        [
            jnp.dot(pick, array, preferred_element_type=F32).astype(BF16)
            for array in (queries, keys, values)
        ]
    )
    counts = jnp.sum(hits, axis=0)
    lanes = -(-n // 128) * 128
    meta = jnp.broadcast_to(jnp.pad(counts, (0, lanes - n))[None, :], (8, lanes))
    return packed, meta


def on_device(
    update_keys,
    update_values,
    update_rates,
    update_mask,
    fast_weights,
    step_sizes,
    target_queries,
    target_keys,
    target_values,
    target_views,
):
    n = lax.axis_size("tokens")
    heads = fast_weights.shape[0]
    width = fast_weights.shape[2]
    me = lax.axis_index("tokens")
    packed, meta = pack_rows(target_queries, target_keys, target_values, target_views, n)
    rates = update_rates * update_mask.astype(F32)[:, None]
    fresh, got, got_meta = exchange(
        update_keys, update_values, rates, fast_weights, step_sizes, packed, meta
    )
    fresh = fresh.reshape(3, width, width)
    rows = target_views.shape[0]
    capacity = 2 * rows // n
    counts = lax.dynamic_slice_in_dim(got_meta[:, 0, :], (me // heads) * heads, heads, 1)
    first = jnp.cumsum(counts, axis=0) - counts
    inside = jnp.arange(capacity, dtype=jnp.int32)
    place_at = jnp.where(
        inside[None, None, :] < counts[:, :, None], first[:, :, None] + inside[None, None, :], -1
    )
    place_at = jnp.transpose(place_at, (1, 0, 2)).reshape(heads, n * capacity)
    place = (
        jnp.arange(rows, dtype=jnp.int32)[None, :, None] == place_at[:, None, :]
    ).astype(BF16)
    got = got.reshape(n, 3, heads, capacity, width)
    got = jnp.transpose(got, (1, 2, 0, 3, 4)).reshape(3, heads, n * capacity, width)
    arranged = jnp.einsum("vrs,cvsd->cvrd", place, got, preferred_element_type=F32).astype(BF16)
    scores = (
        jnp.einsum("vqd,vkd->vqk", arranged[0], arranged[1], preferred_element_type=F32)
        * width ** (-0.5)
    )
    probs = jax.nn.softmax(scores, axis=-1).astype(BF16)
    attended = jnp.einsum("vqk,vkd->vqd", probs, arranged[2], preferred_element_type=F32)
    query_rows = arranged[0].reshape(heads * rows, width)
    pre_gate = jnp.dot(query_rows, fresh[0], preferred_element_type=F32)
    pre_up = jnp.dot(query_rows, fresh[1], preferred_element_type=F32)
    hidden = (pre_gate * jax.nn.sigmoid(pre_gate) * pre_up).astype(BF16)
    fast_out = jnp.dot(hidden, fresh[2], preferred_element_type=F32)
    normed = fast_out * lax.rsqrt(jnp.mean(fast_out * fast_out, axis=-1, keepdims=True) + EPS)
    mixed = (normed.reshape(heads, rows, width) + attended).astype(BF16)
    groups = [[first + i for i in range(heads)] for first in range(0, n, heads)]
    swapped = lax.all_to_all(
        mixed, "tokens", split_axis=0, concat_axis=0, axis_index_groups=groups, tiled=True
    )
    return jnp.transpose(swapped, (1, 0, 2)).reshape(rows, heads * width)


def solution(mesh):
    rows = P(("groups", "tokens"), None)
    flat = P(("groups", "tokens"))
    return jax.shard_map(
        on_device,
        mesh=mesh,
        in_specs=(rows, rows, rows, flat, P(), P(), rows, rows, rows, flat),
        out_specs=rows,
        check_vma=False,
    )
```

time: 330 us -> 191 us (0.58)
  waiting for transfers between devices: 218 us -> 0 us
  Pallas kernels: 0 us -> 149 us
  starting transfers between devices: 31.9 us -> 0 us
  matrix products: 31.3 us -> 12.9 us
  between operations: 13.7 us -> 0.13 us
  blocking collectives: 0 us -> 12.3 us
  local copies, waits for them, and re-layouts: 17.1 us -> 8.43 us
  other arithmetic: 16.1 us -> 7.75 us
    pallas_call x0 -> x1, Pallas kernels: none -> 149 us  [exchange(): pl.pallas_call(functools.partial(exchange_kernel, n, heads), out_shape=(j...]
    reduce_scatter x1 -> x0, waiting for transfers between devices: 137 us -> none  [update_weights(): lax.psum_scatter(grad_local.reshape(flat_rows, head_width), 'tokens', sca...]
    all_to_all x4 -> x0, waiting for transfers between devices: 81.2 us -> none  [the longest x1 31.1 us: regroup_rows(): lax.all_to_all(sent_keys, 'tokens', split_axis=0, concat_axis=0, tiled=True)]
    all_to_all x4 -> x0, starting transfers between devices: 31.9 us -> none  [the longest x1 17.5 us: regroup_rows(): lax.all_to_all(sent_values, 'tokens', split_axis=0, concat_axis=0, tiled=...]
    dot_general x16 -> x9, matrix products: 31.3 us -> 12.9 us  [the longest x1 3.32 us: on_device(): fast_out = jnp.dot(hidden, fresh[2], preferred_element_type=F32)]
    all_to_all x0 -> x1, blocking collectives: none -> 12.3 us  [on_device(): lax.all_to_all(mixed, 'tokens', split_axis=0, concat_axis=0, axis_index_g...]
    another operation x4 -> x0, local copies, waits for them, and re-layouts: 10.9 us -> none  [the longest x1 10.6 us: local_gradient(): return jnp.stack([gate_term, up_term, down_term], axis=1)]
    another operation x4 -> x2, other arithmetic: 11.4 us -> 3.27 us  [the longest x1 3.23 us: pack_rows(): jnp.stack([jnp.dot(pick, array, preferred_element_type=F32).astype(BF16)...]
  transfers between devices with their start and end apart: 6 -> 0, of which waited for: 5 -> 0; matrix products, arithmetic and copies ran while one was open for 3% -> 0% of each run, Pallas kernels for 0% -> 0%
where the time goes in v1:
time: 191 us
  Pallas kernels  149 us (78%)
  matrix products  12.9 us (7%)
  blocking collectives  12.3 us (6%)
  local copies, waits for them, and re-layouts  8.43 us (4%)
  other arithmetic  7.75 us (4%)
    pallas_call x1, Pallas kernels, exchange(): pl.pallas_call(functools.partial(exchange_kernel, n, heads), out_shape=(j...  149 us
    all_to_all x1, blocking collectives, on_device(): lax.all_to_all(mixed, 'tokens', split_axis=0, concat_axis=0, axis_index_g...  12.3 us
    transpose x1, local copies, waits for them, and re-layouts, on_device(): jnp.transpose(got, (1, 2, 0, 3, 4)).reshape(3, heads, n * capacity, width)  3.99 us

profile of v1, /device:TPU:0, one launch (start us, length us, event | category | flops | bytes accessed | tf_op | source)
XLA Modules:
  0.0 190.6 jit_solution(13527842744046132467)
XLA Ops:
  0.0 0.9 copy.27
  1.0 0.7 convert_element_type.38
  1.7 0.8 convert_reduce_fusion
  2.5 1.0 fusion.11
  3.4 0.7 multiply_add_fusion
  4.1 0.4 fusion.3
  4.5 0.4 fusion.2
  5.0 1.4 fusion.1
  6.4 0.8 broadcast_multiply_fusion.1.rates_ref
  7.2 3.2 %pad_maximum_fusion.packed_ref = bf16[3,256,2048]{2,1,0:T(8,128)(2,1)} fusion(bf16[1,256,2048]{2,1,0:T(8,128)(2,1)S(1)} %fusion.3, bf16[1,256,2048]{2,1,0:T(8,128)(2,1)S(1)} %fusion.2, bf16[1,256,2048]{2,1,0:T(8,128)(2,1)} %fusion.1), kind=kLoop, calls=%fused_computation.1 | loop fusion | flops 3145728 | bytes 6291456 | tf_op jit(solution)/shard_map/stack | solution.py:374
  10.5 0.6 broadcast_in_dim.13.meta_ref
  11.0 149.1 %shard_map.100 = (bf16[4,384,512]{2,1,0:T(8,128)(2,1)}, bf16[16,3,64,512]{3,2,1,0:T(8,128)(2,1)}, s32[16,8,128]{2,1,0:T(8,128)}) custom-call(bf16[512,2048]{1,0:T(8,128)(2,1)} %keys_ref.1, bf16[512,2048]{1,0:T(8,128)(2,1)} %values_ref.1, f32[512,4]{1,0:T(8,128)} %broadcast_multiply_fusion.1.rates_ref, bf16[4,3,512,512]{3,2,1,0:T(8,128)(2,1)} %weights_ref.1, ...), custom_call_target="tpu_custom_call" | custom-call | tf_op jit(solution)/shard_map/pallas_call | solution.py:325
  160.2 4.0 %copy.29 = bf16[3,4,16,16,512]{4,3,2,0,1:T(8,128)(2,1)} copy(bf16[3,4,16,16,512]{4,3,1,0,2:T(8,128)(2,1)} %bitcast.60) | data formatting | bytes 6291456 | tf_op jit(solution)/shard_map/transpose | solution.py:421
  164.2 0.8 slice.22
  165.0 0.1 constant_dynamic-slice_fusion
  165.1 0.1 copy.30
  165.2 0.1 copy.31
  165.3 0.1 copy.33
  165.4 0.1 add.60
  165.5 0.1 add.61
  165.6 0.1 lt.44
  165.7 0.1 lt.38
  165.8 2.5 %fusion.4 = bf16[3,4,128,512]{3,2,0,1:T(8,128)(2,1)S(1)} fusion(bf16[3,4,256,512]{3,2,0,1:T(8,128)(2,1)} %bitcast.58, s32[4,256]{1,0:T(4,128)S(1)} %add_select_fusion), kind=kOutput, calls=%fused_computation.9 | convolution fusion | flops 403570688 | bytes 4722688 | tf_op jit(solution)/shard_map/vrs,cvsd->cvrd/dot_general | solution.py:422
  168.3 0.3 convolution_multiply_fusion.1
  168.6 2.5 %fusion.17 = f32[512,512]{1,0:T(8,128)} fusion(bf16[512,512]{1,0:T(8,128)(2,1)S(1)} %bitcast.63, bf16[3,512,512]{2,1,0:T(8,128)(2,1)} %bitcast.65), kind=kOutput, calls=%fused_computation.32 | convolution fusion | flops 268435456 | bytes 2097152 | tf_op jit(solution)/shard_map/dot_general | solution.py:430
  171.1 3.3 %multiply_reduce_fusion = (f32[512]{0:T(512)S(1)}, f32[512,512]{1,0:T(8,128)}) fusion(bf16[3,512,512]{2,1,0:T(8,128)(2,1)} %bitcast.66, bf16[512,512]{1,0:T(8,128)(2,1)S(1)} %bitcast.64, f32[512,512]{1,0:T(8,128)} %fusion.17), kind=kOutput, calls=%fused_computation.21 | convolution fusion | flops 538967552 | bytes 3672064 | tf_op jit(solution)/shard_map/dot_general | solution.py:433
  174.4 0.1 fusion.38
  174.5 1.4 broadcast_multiply_fusion
  175.9 1.2 fusion.6
  177.1 12.3 %all_to_all.5 = bf16[4,128,512]{2,1,0:T(8,128)(2,1)S(1)} all-to-all(bf16[4,128,512]{2,1,0:T(8,128)(2,1)} %fusion.6), channel_id=1, replica_groups={{0,1,2,3},{4,5,6,7},{8,9,10,11},{12,13,14,15},{16,17,18,19},{20,21,22,2..., dimensions={0} | all-to-all | bytes 1048576 | tf_op jit(solution)/shard_map/all_to_all | solution.py:437
  189.3 0.3 copy.35
  189.6 1.0 copy.36
  (15 shorter events, 0.2 us)
Async XLA Ops:
  0.0 4.1 %copy-start = (bf16[128,2048]{1,0:T(8,128)(2,1)S(1)}, bf16[128,2048]{1,0:T(8,128)(2,1)}, u32[]{:S(2)}) copy-start(bf16[128,2048]{1,0:T(8,128)(2,1)} %param.18) | copy-start | bytes 1572868
  0.0 4.5 %copy-start.1 = (bf16[128,2048]{1,0:T(8,128)(2,1)S(1)}, bf16[128,2048]{1,0:T(8,128)(2,1)}, u32[]{:S(2)}) copy-start(bf16[128,2048]{1,0:T(8,128)(2,1)} %param.17) | copy-start | bytes 1572868
  0.9 4.0 %copy-start.2 = (bf16[128,2048]{1,0:T(8,128)(2,1)S(1)}, bf16[128,2048]{1,0:T(8,128)(2,1)}, u32[]{:S(2)}) copy-start(bf16[128,2048]{1,0:T(8,128)(2,1)} %param.16) | copy-start | bytes 1572868

commit v2 on v1

--- a/solution.py
+++ b/solution.py
@@ -3,13 +3,13 @@
 
 import jax
 import jax.numpy as jnp
+import numpy as np
 from jax import lax
 from jax.experimental import pallas as pl
 from jax.experimental.pallas import tpu as pltpu
 from jax.sharding import PartitionSpec as P
 
 EPS = 1e-05
-VIEW_ROWS = 128
 MESH = pl.DeviceIdType.MESH
 F32 = jnp.float32
 BF16 = jnp.bfloat16
@@ -34,11 +34,20 @@
     rates_ref,
     weights_ref,
     steps_ref,
+    queries_ref,
+    view_keys_ref,
+    view_values_ref,
+    views_ref,
+    lanes_ref,
+    out_ref,
     packed_ref,
     meta_ref,
     fresh_ref,
     got_ref,
     got_meta_ref,
+    query_rows,
+    attended,
+    mixed,
     grad,
     core_out,
     core_in,
@@ -58,11 +67,15 @@
     chain_recv,
     spread_send,
     spread_recv,
+    out_send,
+    out_recv,
 ):
     width = weights_ref.shape[-1]
+    rows = queries_ref.shape[0]
     quads = n // heads
     piece = 3 * width // quads
     slots = packed_ref.shape[1] // quads
+    capacity = slots // heads
     me = lax.axis_index("tokens")
     quad = me // heads
     head = me % heads
@@ -76,10 +89,47 @@
         pl.semaphore_signal(
             barrier, inc=1, device_id={"tokens": (me + step) % n}, device_id_type=MESH
         )
+
+    owner = views_ref[0:1, :]
+    hits = lax.broadcasted_iota(jnp.int32, (meta_ref.shape[1], rows), 0) == owner
+    hits = hits.astype(F32).astype(BF16)
+    earlier = (
+        lax.broadcasted_iota(jnp.int32, (rows, rows), 0)
+        < lax.broadcasted_iota(jnp.int32, (rows, rows), 1)
+    ).astype(F32).astype(BF16)
+    before = jnp.dot(hits, earlier, preferred_element_type=F32)
+    rank = jnp.sum(hits.astype(F32) * before, axis=0, keepdims=True).astype(jnp.int32)
+    meta_ref[...] = lax.dot_general(
+        jnp.ones((meta_ref.shape[0], rows), BF16),
+        hits,
+        (((1,), (1,)), ((), ())),
+        preferred_element_type=F32,
+    )
+    pick = (
+        lax.broadcasted_iota(jnp.int32, (n * capacity, rows), 0) == owner * capacity + rank
+    ).astype(F32).astype(BF16)
+    for index, array in enumerate((queries_ref, view_keys_ref, view_values_ref)):
+        packed_ref[index] = jnp.dot(pick, array[...], preferred_element_type=F32).astype(BF16)
+
     pl.semaphore_wait(barrier, n - 1)
 
+    near = [step for step in range(1, n) if step % heads < 2]
+    cross = [step for step in range(1, n) if step % heads >= 2]
+    early = cross[len(cross) // 2 :] + near[::-1]
+    late = cross[: len(cross) // 2][::-1]
+
+    def peer_of(step):
+        place, total = me, 0
+        unit = 1
+        while unit < n:
+            bit = place % 2
+            total = total + unit * ((1 - bit) if (step // unit) % 2 else bit)
+            place = place // 2
+            unit *= 2
+        return total
+
     def block_copy(step):
-        peer = (me + step) % n
+        peer = peer_of(step)
         rows = pl.ds(pl.multiple_of((peer // heads) * slots, slots), slots)
         columns = pl.ds(pl.multiple_of((peer % heads) * width, width), width)
         return remote(
@@ -91,14 +141,14 @@
         )
 
     def meta_copy(step):
-        peer = (me + step) % n
+        peer = peer_of(step)
         return remote(
             meta_ref, got_meta_ref.at[me], meta_send.at[step], meta_recv.at[step], peer
         )
 
     for step in range(1, n):
         meta_copy(step).start()
-    for step in range(1, n):
+    for step in early:
         block_copy(step).start()
     got_meta_ref[me] = meta_ref[...]
     got_ref[me] = packed_ref[
@@ -158,6 +208,8 @@
             core_copy(0).wait_recv()
             side_out[...] = (grad[...] + core_in[0].astype(F32)).astype(BF16)
             side_copy.start()
+            for step in late:
+                block_copy(step).start()
 
         @pl.when(turn == 2)
         def _():
@@ -263,6 +315,46 @@
     def _():
         spread_copy(1, quad).start()
 
+    for step in range(1, n):
+        meta_copy(step).wait()
+        block_copy(step).wait()
+    lane_source, lane_view, lane_slot = (lanes_ref[i : i + 1, :] for i in range(3))
+    lane_count = lanes_ref.shape[1]
+    counts = got_meta_ref[:, 0, :].astype(BF16)
+    sources = lax.broadcasted_iota(jnp.int32, (n, lane_count), 0)
+    over_source = (((0,), (0,)), ((), ()))
+    same = (sources == lane_source).astype(F32).astype(BF16)
+    lower = (sources < lane_source).astype(F32).astype(BF16)
+    owners = lax.broadcasted_iota(jnp.int32, (meta_ref.shape[1], lane_count), 0)
+    wanted = owners == lane_view + quad * heads
+
+    def lane_sum(table):
+        found = lax.dot_general(counts, table, over_source, preferred_element_type=F32)
+        return jnp.sum(jnp.where(wanted, found, 0.0), axis=0, keepdims=True).astype(jnp.int32)
+
+    place_at = jnp.where(
+        lane_slot < lane_sum(same), lane_view * rows + lane_sum(lower) + lane_slot, -1
+    )
+    place = (
+        lax.broadcasted_iota(jnp.int32, (heads * rows, lane_count), 0) == place_at
+    ).astype(F32).astype(BF16)
+    arranged = [
+        jnp.dot(
+            place, got_ref[:, i].reshape(lane_count, width), preferred_element_type=F32
+        ).astype(BF16)
+        for i in range(3)
+    ]
+    for view in range(heads):
+        part = slice(view * rows, (view + 1) * rows)
+        scores = lax.dot_general(
+            arranged[0][part], arranged[1][part], (((1,), (1,)), ((), ())),
+            preferred_element_type=F32,
+        ) * width ** (-0.5)
+        powers = jnp.exp(scores - jnp.max(scores, axis=-1, keepdims=True))
+        probs = (powers / jnp.sum(powers, axis=-1, keepdims=True)).astype(BF16)
+        attended[part] = jnp.dot(probs, arranged[2][part], preferred_element_type=F32)
+    query_rows[...] = arranged[0]
+
     for hop in range(1, quads):
 
         @pl.when(quad - hop >= 0)
@@ -282,6 +374,31 @@
             @pl.when(quad > 0)
             def _():
                 spread_copy(1, index).start()
+
+    fresh = fresh_ref[...].reshape(3 * width, width)
+    pre_gate = jnp.dot(query_rows[...], fresh[0:width], preferred_element_type=F32)
+    pre_up = jnp.dot(query_rows[...], fresh[width : 2 * width], preferred_element_type=F32)
+    target_hidden = (pre_gate * jax.nn.sigmoid(pre_gate) * pre_up).astype(BF16)
+    fast_out = jnp.dot(target_hidden, fresh[2 * width :], preferred_element_type=F32)
+    normed = fast_out * lax.rsqrt(jnp.mean(fast_out * fast_out, axis=-1, keepdims=True) + EPS)
+    mixed[...] = (normed + attended[...]).astype(BF16).reshape(mixed.shape)
+    own_columns = pl.ds(pl.multiple_of(head * width, width), width)
+
+    def out_copy(step):
+        view = (head + step) % heads
+        return remote(
+            mixed.at[view],
+            out_ref.at[:, own_columns],
+            out_send.at[step],
+            out_recv.at[step],
+            quad * heads + view,
+        )
+
+    for step in range(1, heads):
+        out_copy(step).start()
+    out_ref[:, own_columns] = mixed[head]
+    for step in range(1, heads):
+        out_copy(step).wait()
 
     core_copy(0).wait_send()
     core_copy(1).wait_send()
@@ -304,19 +421,22 @@
         def _():
             spread_copy(1, index).wait_send()
 
-    for step in range(1, n):
-        meta_copy(step).wait()
-        block_copy(step).wait()
-
-
-def exchange(keys, values, rates, weights, steps, packed, meta):
+
+def exchange(keys, values, rates, weights, steps, queries, view_keys, view_values, views):
     n = lax.axis_size("tokens")
     heads = weights.shape[0]
     width = weights.shape[-1]
+    rows = queries.shape[0]
     quads = n // heads
     piece = 3 * width // quads
-    slots = packed.shape[1] // quads
-    rows = keys.shape[0]
+    capacity = 2 * rows // n
+    slots = heads * capacity
+    owner_lanes = -(-n // 128) * 128
+    lane = np.arange(n * slots)
+    lanes = np.zeros((8, n * slots), np.int32)
+    lanes[0] = lane // slots
+    lanes[1] = lane % slots // capacity
+    lanes[2] = lane % capacity
     vmem = pl.BlockSpec(memory_space=pltpu.VMEM)
     smem = pl.BlockSpec(memory_space=pltpu.SMEM)
     dma = pltpu.SemaphoreType.DMA
@@ -324,14 +444,18 @@
     parts = (quads, piece, width)
     return pl.pallas_call(
         functools.partial(exchange_kernel, n, heads),
-        out_shape=(
-            jax.ShapeDtypeStruct(parts, BF16),
-            jax.ShapeDtypeStruct((n, 3, slots, width), BF16),
-            jax.ShapeDtypeStruct((n,) + meta.shape, jnp.int32),
-        ),
-        in_specs=[vmem, vmem, vmem, vmem, smem, vmem, vmem],
-        out_specs=(vmem, vmem, vmem),
+        out_shape=jax.ShapeDtypeStruct((rows, heads * width), BF16),
+        in_specs=[vmem, vmem, vmem, vmem, smem] + [vmem] * 5,
+        out_specs=vmem,
         scratch_shapes=[
+            pltpu.VMEM((3, n * capacity, heads * width), BF16),
+            pltpu.VMEM((8, owner_lanes), F32),
+            pltpu.VMEM(parts, BF16),
+            pltpu.VMEM((n, 3, slots, width), BF16),
+            pltpu.VMEM((n, 8, owner_lanes), F32),
+            pltpu.VMEM((heads * rows, width), BF16),
+            pltpu.VMEM((heads * rows, width), F32),
+            pltpu.VMEM((heads, rows, width), BF16),
             pltpu.VMEM(whole, F32),
             pltpu.VMEM((2,) + whole, BF16),
             pltpu.VMEM((2,) + whole, BF16),
@@ -351,36 +475,13 @@
             dma((2, quads)),
             dma((2, quads)),
             dma((quads,)),
+            dma((heads,)),
+            dma((heads,)),
         ],
         compiler_params=pltpu.CompilerParams(
             collective_id=0, has_side_effects=True, vmem_limit_bytes=63 * 1024 * 1024
         ),
-    )(keys, values, rates, weights, steps, packed, meta)
-
-
-def pack_rows(queries, keys, values, views, n):
-    rows = views.shape[0]
-    capacity = 2 * rows // n
-    hits = (views[:, None] // (rows // VIEW_ROWS) == jnp.arange(n, dtype=jnp.int32)[None, :]).astype(
-        jnp.int32
-    )
-    before = jnp.tril(jnp.ones((rows, rows), BF16), -1)
-    rank = jnp.sum(
-        hits * jnp.dot(before, hits.astype(BF16), preferred_element_type=F32).astype(jnp.int32),
-        axis=1,
-    )
-    slot = (views // (rows // VIEW_ROWS)) * capacity + rank
-    pick = (jnp.arange(n * capacity, dtype=jnp.int32)[:, None] == slot[None, :]).astype(BF16)
-    packed = jnp.stack(
-        [
-            jnp.dot(pick, array, preferred_element_type=F32).astype(BF16)
-            for array in (queries, keys, values)
-        ]
-    )
-    counts = jnp.sum(hits, axis=0)
-    lanes = -(-n // 128) * 128
-    meta = jnp.broadcast_to(jnp.pad(counts, (0, lanes - n))[None, :], (8, lanes))
-    return packed, meta
+    )(keys, values, rates, weights, steps, queries, view_keys, view_values, views, jnp.asarray(lanes))
 
 
 def on_device(
@@ -395,49 +496,18 @@
     target_values,
     target_views,
 ):
-    n = lax.axis_size("tokens")
-    heads = fast_weights.shape[0]
-    width = fast_weights.shape[2]
-    me = lax.axis_index("tokens")
-    packed, meta = pack_rows(target_queries, target_keys, target_values, target_views, n)
     rates = update_rates * update_mask.astype(F32)[:, None]
-    fresh, got, got_meta = exchange(
-        update_keys, update_values, rates, fast_weights, step_sizes, packed, meta
+    return exchange(
+        update_keys,
+        update_values,
+        rates,
+        fast_weights,
+        step_sizes,
+        target_queries,
+        target_keys,
+        target_values,
+        target_views[None, :],
     )
-    fresh = fresh.reshape(3, width, width)
-    rows = target_views.shape[0]
-    capacity = 2 * rows // n
-    counts = lax.dynamic_slice_in_dim(got_meta[:, 0, :], (me // heads) * heads, heads, 1)
-    first = jnp.cumsum(counts, axis=0) - counts
-    inside = jnp.arange(capacity, dtype=jnp.int32)
-    place_at = jnp.where(
-        inside[None, None, :] < counts[:, :, None], first[:, :, None] + inside[None, None, :], -1
-    )
-    place_at = jnp.transpose(place_at, (1, 0, 2)).reshape(heads, n * capacity)
-    place = (
-        jnp.arange(rows, dtype=jnp.int32)[None, :, None] == place_at[:, None, :]
-    ).astype(BF16)
-    got = got.reshape(n, 3, heads, capacity, width)
-    got = jnp.transpose(got, (1, 2, 0, 3, 4)).reshape(3, heads, n * capacity, width)
-    arranged = jnp.einsum("vrs,cvsd->cvrd", place, got, preferred_element_type=F32).astype(BF16)
-    scores = (
-        jnp.einsum("vqd,vkd->vqk", arranged[0], arranged[1], preferred_element_type=F32)
-        * width ** (-0.5)
-    )
-    probs = jax.nn.softmax(scores, axis=-1).astype(BF16)
-    attended = jnp.einsum("vqk,vkd->vqd", probs, arranged[2], preferred_element_type=F32)
-    query_rows = arranged[0].reshape(heads * rows, width)
-    pre_gate = jnp.dot(query_rows, fresh[0], preferred_element_type=F32)
-    pre_up = jnp.dot(query_rows, fresh[1], preferred_element_type=F32)
-    hidden = (pre_gate * jax.nn.sigmoid(pre_gate) * pre_up).astype(BF16)
-    fast_out = jnp.dot(hidden, fresh[2], preferred_element_type=F32)
-    normed = fast_out * lax.rsqrt(jnp.mean(fast_out * fast_out, axis=-1, keepdims=True) + EPS)
-    mixed = (normed.reshape(heads, rows, width) + attended).astype(BF16)
-    groups = [[first + i for i in range(heads)] for first in range(0, n, heads)]
-    swapped = lax.all_to_all(
-        mixed, "tokens", split_axis=0, concat_axis=0, axis_index_groups=groups, tiled=True
-    )
-    return jnp.transpose(swapped, (1, 0, 2)).reshape(rows, heads * width)
 
 
 def solution(mesh):

time: 191 us -> 157 us (0.82)
  matrix products: 12.9 us -> 0 us
  blocking collectives: 12.3 us -> 0 us
  other arithmetic: 7.75 us -> 1.53 us
  local copies, waits for them, and re-layouts: 8.43 us -> 2.72 us
  Pallas kernels: 149 us -> 152 us
    dot_general x9 -> x0, matrix products: 12.9 us -> none  [the longest x1 3.32 us: on_device(): fast_out = jnp.dot(hidden, fresh[2], preferred_element_type=F32)]
    all_to_all x1 -> x0, blocking collectives: 12.3 us -> none  [on_device(): lax.all_to_all(mixed, 'tokens', split_axis=0, concat_axis=0, axis_index_g...]
    transpose x2 -> x0, local copies, waits for them, and re-layouts: 4.26 us -> none  [the longest x1 3.99 us: on_device(): jnp.transpose(got, (1, 2, 0, 3, 4)).reshape(3, heads, n * capacity, width)]
    another operation x2 -> x0, other arithmetic: 3.27 us -> none  [the longest x1 3.23 us: pack_rows(): jnp.stack([jnp.dot(pick, array, preferred_element_type=F32).astype(BF16)...]
    pallas_call x1, Pallas kernels: 149 us -> 152 us  [exchange(): pl.pallas_call(functools.partial(exchange_kernel, n, heads), out_shape=ja...]
where the time goes in v2:
time: 157 us; the launch traced here: 156 us
  Pallas kernels  152 us (97%)
  local copies, waits for them, and re-layouts  2.72 us (2%)
    pallas_call x1, Pallas kernels, exchange(): pl.pallas_call(functools.partial(exchange_kernel, n, heads), out_shape=ja...  152 us

profile of v2, /device:TPU:0, one launch (start us, length us, event | category | flops | bytes accessed | tf_op | source)
XLA Modules:
  0.0 156.2 jit_solution(8873724745855347024)
XLA Ops:
  0.0 0.7 convert_element_type.3
  0.7 0.8 copy.13
  1.5 0.8 broadcast_multiply_fusion.rates_ref
  2.4 152.0 %shard_map.109 = bf16[128,2048]{1,0:T(8,128)(2,1)} custom-call(bf16[512,2048]{1,0:T(8,128)(2,1)} %keys_ref.1, bf16[512,2048]{1,0:T(8,128)(2,1)} %values_ref.1, f32[512,4]{1,0:T(8,128)} %broadcast_multiply_fusion.rates_ref, bf16[4,3,512,512]{3,2,1,0:T(8,128)(2,1)} %weights_ref.1, f32[4]{0:T(128)} %steps_ref.1, bf16[128,2048]{1,0:T(8,128)(2,1)} %queries_ref.1, ...), custom_call_target="tpu_custom_call" | custom-call | tf_op jit(solution)/shard_map/pallas_call | solution.py:445
  154.4 1.9 %copy.16 = bf16[128,2048]{1,0:T(8,128)(2,1)} copy(bf16[128,2048]{1,0:T(8,128)(2,1)} %shard_map.109) | data formatting | bytes 1048576

commit v3 on v2

--- a/solution.py
+++ b/solution.py
@@ -115,8 +115,8 @@
 
     near = [step for step in range(1, n) if step % heads < 2]
     cross = [step for step in range(1, n) if step % heads >= 2]
-    early = cross[len(cross) // 2 :] + near[::-1]
-    late = cross[: len(cross) // 2][::-1]
+    early = near[::-1]
+    late = cross[::-1]
 
     def peer_of(step):
         place, total = me, 0
@@ -246,31 +246,41 @@
             me - heads,
         )
 
-    for turn in range(quads - 1):
-        high = quads - 1 - turn
-        low = turn
-
+    def send_up(index):
         @pl.when(quad == 0)
         def _():
-            up_out[high] = own_part(rows_of(high)).astype(BF16)
-            up_copy(high).start()
-
+            up_out[index] = own_part(rows_of(index)).astype(BF16)
+            up_copy(index).start()
+
+        @pl.when((quad > 0) & (quad < index))
+        def _():
+            up_copy(index).wait_recv()
+            up_out[index] = (own_part(rows_of(index)) + up_in[index].astype(F32)).astype(BF16)
+            up_copy(index).start()
+
+    def send_down(index):
         @pl.when(quad == quads - 1)
         def _():
-            down_out[low] = own_part(rows_of(low)).astype(BF16)
-            down_copy(low).start()
-
-        @pl.when((quad > 0) & (quad < high))
-        def _():
-            up_copy(high).wait_recv()
-            up_out[high] = (own_part(rows_of(high)) + up_in[high].astype(F32)).astype(BF16)
-            up_copy(high).start()
-
-        @pl.when((quad < quads - 1) & (quad > low))
-        def _():
-            down_copy(low).wait_recv()
-            down_out[low] = (own_part(rows_of(low)) + down_in[low].astype(F32)).astype(BF16)
-            down_copy(low).start()
+            down_out[index] = own_part(rows_of(index)).astype(BF16)
+            down_copy(index).start()
+
+        @pl.when((quad < quads - 1) & (quad > index))
+        def _():
+            down_copy(index).wait_recv()
+            down_out[index] = (own_part(rows_of(index)) + down_in[index].astype(F32)).astype(BF16)
+            down_copy(index).start()
+
+    @pl.when(2 * quad < quads)
+    def _():
+        for turn in range(quads - 1):
+            send_up(quads - 1 - turn)
+            send_down(turn)
+
+    @pl.when(2 * quad >= quads)
+    def _():
+        for turn in range(quads - 1):
+            send_down(turn)
+            send_up(quads - 1 - turn)
 
     mine = pl.ds(pl.multiple_of(quad * piece, piece), piece)
     grad[mine, :] = own_part(mine)

time: 157 us -> 137 us (0.87)
  Pallas kernels: 152 us -> 132 us
    pallas_call x1, Pallas kernels: 152 us -> 132 us  [exchange(): pl.pallas_call(functools.partial(exchange_kernel, n, heads), out_shape=ja...]
where the time goes in v3:
time: 137 us; the launch traced here: 136 us
  Pallas kernels  132 us (96%)
  local copies, waits for them, and re-layouts  2.72 us (2%)
  other arithmetic  1.53 us (1%)
    pallas_call x1, Pallas kernels, exchange(): pl.pallas_call(functools.partial(exchange_kernel, n, heads), out_shape=ja...  132 us

profile of v3, /device:TPU:0, one launch (start us, length us, event | category | flops | bytes accessed | tf_op | source)
XLA Modules:
  0.0 136.5 jit_solution(12476357546011960079)
XLA Ops:
  0.0 0.7 convert_element_type.3
  0.7 0.8 copy.13
  1.5 0.8 broadcast_multiply_fusion.rates_ref
  2.4 132.2 %shard_map.109 = bf16[128,2048]{1,0:T(8,128)(2,1)} custom-call(bf16[512,2048]{1,0:T(8,128)(2,1)} %keys_ref.1, bf16[512,2048]{1,0:T(8,128)(2,1)} %values_ref.1, f32[512,4]{1,0:T(8,128)} %broadcast_multiply_fusion.rates_ref, bf16[4,3,512,512]{3,2,1,0:T(8,128)(2,1)} %weights_ref.1, f32[4]{0:T(128)} %steps_ref.1, bf16[128,2048]{1,0:T(8,128)(2,1)} %queries_ref.1, ...), custom_call_target="tpu_custom_call" | custom-call | tf_op jit(solution)/shard_map/pallas_call | solution.py:455
  134.6 1.9 %copy.16 = bf16[128,2048]{1,0:T(8,128)(2,1)} copy(bf16[128,2048]{1,0:T(8,128)(2,1)} %shard_map.109) | data formatting | bytes 1048576

commit v4 on v3

--- a/solution.py
+++ b/solution.py
@@ -63,6 +63,8 @@
     meta_recv,
     pair_send,
     pair_recv,
+    side_send,
+    side_recv,
     chain_send,
     chain_recv,
     spread_send,
@@ -116,7 +118,7 @@
     near = [step for step in range(1, n) if step % heads < 2]
     cross = [step for step in range(1, n) if step % heads >= 2]
     early = near[::-1]
-    late = cross[::-1]
+    late = cross
 
     def peer_of(step):
         place, total = me, 0
@@ -162,7 +164,29 @@
             core_out.at[slot], core_in.at[slot], pair_send.at[slot], pair_recv.at[slot], core_peer
         )
 
-    side_copy = remote(side_out, side_in, pair_send.at[2], pair_recv.at[2], side_peer)
+    def side_copy(index):
+        part = pl.ds(index * piece, piece)
+        return remote(
+            side_out.at[part, :],
+            side_in.at[part, :],
+            side_send.at[index],
+            side_recv.at[index],
+            side_peer,
+        )
+
+    falling = list(range(quads))[::-1]
+    rising = falling[::-1]
+
+    def mixed_order(first, second):
+        both = [index for pair in zip(first, second) for index in pair]
+        return list(dict.fromkeys(both))
+
+    side_orders = (
+        (quad == 0, falling),
+        (quad == quads - 1, rising),
+        ((quad > 0) & (2 * quad < quads), mixed_order(falling, rising)),
+        ((quad < quads - 1) & (2 * quad >= quads), mixed_order(rising, falling)),
+    )
 
     def one_head(turn, carry):
         on_side = jnp.where(turn < 2, 1 - side, side)
@@ -207,7 +231,13 @@
         def _():
             core_copy(0).wait_recv()
             side_out[...] = (grad[...] + core_in[0].astype(F32)).astype(BF16)
-            side_copy.start()
+            for chosen, order in side_orders:
+
+                @pl.when(chosen)
+                def _(order=order):
+                    for index in order:
+                        side_copy(index).start()
+
             for step in late:
                 block_copy(step).start()
 
@@ -220,12 +250,12 @@
 
     lax.fori_loop(0, 4, one_head, 0)
     core_copy(1).wait_recv()
-    side_copy.wait_recv()
 
     def rows_of(index):
         return pl.ds(index * piece, piece)
 
-    def own_part(rows):
+    def own_part(index, rows):
+        side_copy(index).wait_recv()
         return grad[rows, :] + core_in[1, rows, :].astype(F32) + side_in[rows, :].astype(F32)
 
     def up_copy(index):
@@ -249,25 +279,25 @@
     def send_up(index):
         @pl.when(quad == 0)
         def _():
-            up_out[index] = own_part(rows_of(index)).astype(BF16)
+            up_out[index] = own_part(index, rows_of(index)).astype(BF16)
             up_copy(index).start()
 
         @pl.when((quad > 0) & (quad < index))
         def _():
             up_copy(index).wait_recv()
-            up_out[index] = (own_part(rows_of(index)) + up_in[index].astype(F32)).astype(BF16)
+            up_out[index] = (own_part(index, rows_of(index)) + up_in[index].astype(F32)).astype(BF16)
             up_copy(index).start()
 
     def send_down(index):
         @pl.when(quad == quads - 1)
         def _():
-            down_out[index] = own_part(rows_of(index)).astype(BF16)
+            down_out[index] = own_part(index, rows_of(index)).astype(BF16)
             down_copy(index).start()
 
         @pl.when((quad < quads - 1) & (quad > index))
         def _():
             down_copy(index).wait_recv()
-            down_out[index] = (own_part(rows_of(index)) + down_in[index].astype(F32)).astype(BF16)
+            down_out[index] = (own_part(index, rows_of(index)) + down_in[index].astype(F32)).astype(BF16)
             down_copy(index).start()
 
     @pl.when(2 * quad < quads)
@@ -283,7 +313,7 @@
             send_up(quads - 1 - turn)
 
     mine = pl.ds(pl.multiple_of(quad * piece, piece), piece)
-    grad[mine, :] = own_part(mine)
+    grad[mine, :] = own_part(quad, mine)
 
     @pl.when(quad > 0)
     def _():
@@ -324,6 +354,26 @@
     @pl.when(quad > 0)
     def _():
         spread_copy(1, quad).start()
+
+    for hop in range(1, quads):
+
+        @pl.when(quad - hop >= 0)
+        def _():
+            index = quad - hop
+            spread_copy(0, index).wait_recv()
+
+            @pl.when(quad < quads - 1)
+            def _():
+                spread_copy(0, index).start()
+
+        @pl.when(quad + hop < quads)
+        def _():
+            index = quad + hop
+            spread_copy(1, index).wait_recv()
+
+            @pl.when(quad > 0)
+            def _():
+                spread_copy(1, index).start()
 
     for step in range(1, n):
         meta_copy(step).wait()
@@ -365,26 +415,6 @@
         attended[part] = jnp.dot(probs, arranged[2][part], preferred_element_type=F32)
     query_rows[...] = arranged[0]
 
-    for hop in range(1, quads):
-
-        @pl.when(quad - hop >= 0)
-        def _():
-            index = quad - hop
-            spread_copy(0, index).wait_recv()
-
-            @pl.when(quad < quads - 1)
-            def _():
-                spread_copy(0, index).start()
-
-        @pl.when(quad + hop < quads)
-        def _():
-            index = quad + hop
-            spread_copy(1, index).wait_recv()
-
-            @pl.when(quad > 0)
-            def _():
-                spread_copy(1, index).start()
-
     fresh = fresh_ref[...].reshape(3 * width, width)
     pre_gate = jnp.dot(query_rows[...], fresh[0:width], preferred_element_type=F32)
     pre_up = jnp.dot(query_rows[...], fresh[width : 2 * width], preferred_element_type=F32)
@@ -412,7 +442,8 @@
 
     core_copy(0).wait_send()
     core_copy(1).wait_send()
-    side_copy.wait_send()
+    for index in range(quads):
+        side_copy(index).wait_send()
     for index in range(quads):
 
         @pl.when(quad < index)
@@ -479,8 +510,10 @@
             dma((n,)),
             dma((n,)),
             dma((n,)),
-            dma((3,)),
-            dma((3,)),
+            dma((2,)),
+            dma((2,)),
+            dma((quads,)),
+            dma((quads,)),
             dma((2, quads)),
             dma((2, quads)),
             dma((2, quads)),

time: 137 us -> 141 us (1.029)
  Pallas kernels: 132 us -> 136 us
    pallas_call x1, Pallas kernels: 132 us -> 136 us  [exchange(): pl.pallas_call(functools.partial(exchange_kernel, n, heads), out_shape=ja...]
where the time goes in v4:
time: 141 us
  Pallas kernels  136 us (96%)
  local copies, waits for them, and re-layouts  2.72 us (2%)
  other arithmetic  1.53 us (1%)
    pallas_call x1, Pallas kernels, exchange(): pl.pallas_call(functools.partial(exchange_kernel, n, heads), out_shape=ja...  136 us

profile of v4, /device:TPU:0, one launch (start us, length us, event | category | flops | bytes accessed | tf_op | source)
XLA Modules:
  0.0 140.6 jit_solution(10035892957392165077)
XLA Ops:
  0.0 0.7 convert_element_type.3
  0.7 0.8 copy.13
  1.5 0.8 broadcast_multiply_fusion.rates_ref
  2.4 136.3 %shard_map.109 = bf16[128,2048]{1,0:T(8,128)(2,1)} custom-call(bf16[512,2048]{1,0:T(8,128)(2,1)} %keys_ref.1, bf16[512,2048]{1,0:T(8,128)(2,1)} %values_ref.1, f32[512,4]{1,0:T(8,128)} %broadcast_multiply_fusion.rates_ref, bf16[4,3,512,512]{3,2,1,0:T(8,128)(2,1)} %weights_ref.1, f32[4]{0:T(128)} %steps_ref.1, bf16[128,2048]{1,0:T(8,128)(2,1)} %queries_ref.1, ...), custom_call_target="tpu_custom_call" | custom-call | tf_op jit(solution)/shard_map/pallas_call | solution.py:486
  138.7 1.9 %copy.16 = bf16[128,2048]{1,0:T(8,128)(2,1)} copy(bf16[128,2048]{1,0:T(8,128)(2,1)} %shard_map.109) | data formatting | bytes 1048576
